TPU v7x, 32 devices: a whole 2x2x4 slice. The times are simulated.
32 devices in a mesh: pipe: 2 (over y), ctx: 4 (over x, core), dp: 4 (over z).
Axes of the slice: x: 2, y: 2, z: 4, core: 2. Of those that a mesh axis runs over, the one named last changes fastest.
Arguments:
- hidden_in: bfloat16 [2, 4, 2048, 3584], P('pipe', 'dp', 'ctx'), may hold values from -6 to 6
- selected: int32 [2, 4, 32, 16], P('pipe', 'dp', 'ctx'), may hold values from -1 to 31, as said below
- norm_gain: float32 [2, 3584], P('pipe'), may hold values from 0.1 to 1.9
- kv_weight: bfloat16 [2, 3584, 512], P('pipe', ('ctx', 'dp')), may hold values from -0.1875 to 0.1875
- gate_weight: bfloat16 [2, 28, 3584], P('pipe'), may hold values from -0.09375 to 0.09375
- saved_norm: bfloat16 [2, 4, 2048, 3584], P('pipe', 'dp', 'ctx'), may hold values from -6 to 6
- kv_cot: bfloat16 [2, 4, 2048, 512], P('pipe', 'dp', 'ctx'), may hold values from -0.15625 to 0.15625
- gate_cot: bfloat16 [2, 4, 2048, 28], P('pipe', 'dp', 'ctx'), may hold values from -0.15625 to 0.15625
Outputs:
- passed: bfloat16 [2, 4, 2048, 3584], P('pipe', 'dp', 'ctx')
- kv_grad: bfloat16 [2, 3584, 512], P('pipe', ('ctx', 'dp'))
- gate_grad: bfloat16 [2, 28, 3584], P('pipe', None, ('ctx', 'dp'))
Inputs may be any that keep to these rules, and one draw needn't show every extreme that they name: `selected`: for query block b, entry 0 is b; then come min(b, 15) distinct blocks below b in random order, then -1 in the remaining entries.
All inputs are finite; a program needn't handle non-finite values.
Results may differ from a plain program's by a relative error of at most 0.0061.
Values may be sent and summed in bfloat16 or wider, within the bound.
A program may use at most 128 MiB of HBM per device.

v0:
```python
import math
import jax
import jax.numpy as jnp
from jax import lax
from jax.sharding import PartitionSpec as P

H = 28
HD = 128
KVH = 2
BLOCK = 64
SEL = 16
epsilon = 1e-06


def passed_along(block, axis, distance):
    devices = range(lax.axis_size(axis))
    route = [((i - distance) % len(devices), i) for i in devices]
    return lax.ppermute(block, axis, route)


def attend_block(packed, key_rows, value_rows):
    query_block, block_picks, block_place = packed
    group = H // KVH
    chosen = jnp.maximum(block_picks, 0)
    key_tiles = jnp.take(key_rows, chosen, axis=0).reshape(SEL * BLOCK, KVH, HD)
    value_tiles = jnp.take(value_rows, chosen, axis=0).reshape(SEL * BLOCK, KVH, HD)
    query_heads = query_block.reshape(BLOCK, KVH, group, HD)
    score_scale = 1.0 / math.sqrt(HD)
    scores = (
        jnp.einsum("qgjd,kgd->gjqk", query_heads, key_tiles, preferred_element_type=jnp.float32)
        * score_scale
    )
    key_place = (chosen[:, None] * BLOCK + jnp.arange(BLOCK, dtype=jnp.int32)[None, :]).reshape(-1)
    present = jnp.broadcast_to((block_picks >= 0)[:, None], (SEL, BLOCK)).reshape(-1)
    query_place = block_place * BLOCK + jnp.arange(BLOCK, dtype=jnp.int32)
    allowed = present[None, :] & (key_place[None, :] <= query_place[:, None])
    scores = jnp.where(allowed, scores, -1e30)
    row_max = jnp.max(scores, axis=-1, keepdims=True)
    weights = jnp.exp(scores - row_max)
    denominator = jnp.sum(weights, axis=-1)
    weights_low = weights.astype(jnp.bfloat16)
    blended = jnp.einsum(
        "gjqk,kgd->qgjd", weights_low, value_tiles, preferred_element_type=jnp.float32
    )
    blended = blended / jnp.transpose(denominator, (2, 0, 1))[..., None]
    return blended.reshape(BLOCK, H * HD)


def per_device(
    hidden_in, selected, norm_gain, kv_weight, gate_weight, saved_norm, kv_cot, gate_cot
):
    current = hidden_in[0, 0]
    picks = selected[0, 0]
    length = current.shape[0]
    hidden = current.astype(jnp.float32)
    normed = (
        hidden
        * lax.rsqrt(jnp.mean(hidden * hidden, axis=-1, keepdims=True) + epsilon)
        * norm_gain[0]
    ).astype(jnp.bfloat16)
    projected = jnp.dot(
        normed,
        lax.all_gather(kv_weight[0], ("ctx", "dp"), axis=0, tiled=True),
        preferred_element_type=jnp.float32,
    ).astype(jnp.bfloat16)
    sequence_kv = lax.all_gather(projected, "ctx", axis=0, tiled=True)
    half_width = KVH * HD
    blocks_all = sequence_kv.shape[0] // BLOCK
    key_rows = sequence_kv[:, :half_width].reshape(blocks_all, BLOCK, KVH, HD)
    value_rows = sequence_kv[:, half_width:].reshape(blocks_all, BLOCK, KVH, HD)
    gating = jax.nn.sigmoid(
        lax.dot_general(
            normed, gate_weight[0], (((1,), (1,)), ((), ())), preferred_element_type=jnp.float32
        )
    )
    blocks_here = length // BLOCK
    places = lax.axis_index("ctx") * blocks_here + jnp.arange(blocks_here, dtype=jnp.int32)
    attended = lax.map(
        lambda packed: attend_block(packed, key_rows, value_rows),
        (normed.reshape(blocks_here, BLOCK, H * HD), picks, places),
    )
    attended = attended.reshape(length, H, HD)
    section_out = hidden.reshape(length, H, HD) + gating[:, :, None] * attended
    section_out = section_out.reshape(length, H * HD).astype(jnp.bfloat16)
    passed = passed_along(section_out[None, None], "pipe", 1)
    saved_rows = saved_norm[0, 0]
    local_kv = lax.dot_general(
        saved_rows, kv_cot[0, 0], (((0,), (0,)), ((), ())), preferred_element_type=jnp.float32
    )
    local_gate = lax.dot_general(
        gate_cot[0, 0], saved_rows, (((0,), (0,)), ((), ())), preferred_element_type=jnp.float32
    )
    summed_kv = lax.psum_scatter(local_kv, ("ctx", "dp"), scatter_dimension=0, tiled=True)
    summed_gate = lax.psum_scatter(local_gate, ("ctx", "dp"), scatter_dimension=1, tiled=True)
    kv_grad = summed_kv[None].astype(jnp.bfloat16)
    gate_grad = summed_gate[None].astype(jnp.bfloat16)
    return (passed, kv_grad, gate_grad)


def solution(mesh):
    in_specs = (
        P("pipe", "dp", "ctx", None),
        P("pipe", "dp", "ctx", None),
        P("pipe", None),
        P("pipe", ("ctx", "dp"), None),
        P("pipe", None, None),
        P("pipe", "dp", "ctx", None),
        P("pipe", "dp", "ctx", None),
        P("pipe", "dp", "ctx", None),
    )
    out_specs = (
        P("pipe", "dp", "ctx", None),
        P("pipe", ("ctx", "dp"), None),
        P("pipe", None, ("ctx", "dp")),
    )
    return jax.shard_map(
        per_device, mesh=mesh, in_specs=in_specs, out_specs=out_specs, check_vma=False
    )
```

profile of v0, /device:TPU:0, one launch (start us, length us, event | category | flops | bytes accessed | tf_op | source)
XLA Modules:
  0.0 360.6 jit_solution(8013587021462063414)
XLA Ops:
  8.0 5.9 %copy.34 = bf16[1,1,512,3584]{2,3,1,0:T(8,128)(2,1)} copy(bf16[1,1,512,3584]{3,2,1,0:T(8,128)(2,1)} %param.12) | data formatting | bytes 7340032 | tf_op args[0]
  13.9 2.9 fusion.18
  16.8 43.9 %all-gather.6.cloned.1.call-done = bf16[1,3584,512]{2,1,0:T(8,128)(2,1)} async-done(((bf16[1,224,512]{2,1,0:T(8,128)(2,1)}), bf16[1,3584,512]{2,1,0:T(8,128)(2,1)}) %all-gather.6.cloned.1.call-update) | async-done | bytes 3670032 | tf_op jit(solution)/shard_map/all_gather | solution.py:63
  60.7 6.2 %fusion.34 = bf16[512,512]{1,0:T(8,128)(2,1)} fusion(bf16[1,3584,512]{2,1,0:T(8,128)(2,1)} %all-gather.6.cloned.1.call-done, bf16[1,1,512,3584]{2,3,1,0:T(8,128)(2,1)} %copy.34, f32[3584]{0:T(1024)S(1)} %reduce, f32[512]{0:T(512)S(1)} %add_rsqrt_fusion), kind=kOutput, calls=%fused_computation.50 | convolution fusion | flops 1886650368 | bytes 7880704 | tf_op jit(solution)/shard_map/dot_general | solution.py:61
  67.0 4.8 %convolution_bitcast_fusion = f32[3584,28]{1,0:T(8,128)} fusion(bf16[1,1,512,3584]{3,2,1,0:T(8,128)(2,1)} %param.17, bf16[1,1,512,28]{2,3,1,0:T(8,128)(2,1)S(1)} %copy-done.4), kind=kOutput, calls=%fused_computation.38 | convolution fusion | flops 102760448 | bytes 4100096
  71.9 7.4 %fusion.27 = f32[3584,512]{1,0:T(8,128)} fusion(bf16[1,1,512,3584]{3,2,1,0:T(8,128)(2,1)} %param.17, bf16[1,1,512,512]{3,2,1,0:T(8,128)(2,1)S(1)} %copy-done), kind=kOutput, calls=%fused_computation.43 | convolution fusion | flops 1879048192 | bytes 11534336 | tf_op jit(solution)/shard_map/dot_general | solution.py:87
  79.5 6.3 %copy.35 = f32[1,1,512,3584]{3,2,1,0:T(8,128)} copy(bf16[1,1,512,3584]{2,3,1,0:T(8,128)(2,1)} %copy.34) | data formatting | bytes 11010048 | tf_op jit(solution)/shard_map/convert_element_type | solution.py:55
  85.8 4.0 %fusion.48 = f32[512,28]{0,1:T(8,128)} fusion(bf16[1,1,512,3584]{2,3,1,0:T(8,128)(2,1)} %copy.34, f32[3584]{0:T(1024)S(1)} %reduce, f32[512]{0:T(512)S(1)} %add_rsqrt_fusion, bf16[1,28,3584]{2,1,0:T(8,128)(2,1)S(1)} %copy-done.6), kind=kOutput, calls=%fused_computation.54 | convolution fusion | flops 110143488 | bytes 3944448 | tf_op jit(solution)/shard_map/dot_general | solution.py:72
  89.8 6.1 %multiply_convert_fusion = bf16[8,64,3584]{2,1,0:T(8,128)(2,1)} fusion(f32[8,64,3584]{2,1,0:T(8,128)} %bitcast.106, f32[3584]{0:T(1024)S(1)} %reduce, f32[8,64]{1,0:T(8,128)S(1)} %rsqrt.13), kind=kLoop, calls=%fused_computation.36 | loop fusion | flops 5505024 | bytes 11026432 | tf_op jit(solution)/shard_map/convert_element_type | solution.py:60
  95.8 2.7 fusion.54
  101.0 143.4 %while.10 = (s32[]{:T(128)}, f32[8,64,3584]{2,1,0:T(8,128)}, s32[8,16]{1,0:T(8,128)}, bf16[32,64,2,128]{3,2,1,0:T(2,128)(2,1)S(1)}, s32[8]{0:T(128)S(1)}, /*inde...) while((s32[]{:T(128)}, f32[8,64,3584]{2,1,0:T(8,128)}, ...), condition=%wide.region_4.6_spmd, body=%wide.region_1.5_spmd.sunk | while | flops 960592640 | bytes 36303624 | solution.py:78
  103.3 2.9 gather_fusion.1
  115.2 2.0 fusion.64
  121.3 2.8 gather_fusion.1
  133.1 2.0 fusion.64
  139.2 2.9 gather_fusion.1
  151.1 2.0 fusion.64
  157.1 2.8 gather_fusion.1
  169.0 2.0 fusion.64
  175.1 2.9 gather_fusion.1
  187.0 2.0 fusion.64
  193.0 2.8 gather_fusion.1
  204.8 2.0 fusion.64
  210.9 2.9 gather_fusion.1
  222.7 2.0 fusion.64
  228.9 2.8 gather_fusion.1
  240.7 2.0 fusion.64
  244.5 8.4 %copy.36 = f32[1,1,512,3584]{2,3,1,0:T(8,128)} copy(f32[1,1,512,3584]{3,2,1,0:T(8,128)} %bitcast.109) | data formatting | bytes 14680064 | tf_op jit(solution)/shard_map/reshape | solution.py:82
  252.9 3.9 %mul.88 = f32[512,28,128]{0,2,1:T(8,128)} broadcast(f32[512,28]{0,1:T(8,128)S(1)} %copy-done.3), dimensions={0,1} | broadcast | bytes 7397376 | tf_op jit(solution)/shard_map/mul | solution.py:83
  256.8 9.6 %add_convert_fusion = bf16[1,1,512,3584]{2,3,1,0:T(8,128)(2,1)} fusion(f32[1,1,512,3584]{2,3,1,0:T(8,128)} %bitcast.107, f32[1,1,512,3584]{2,3,1,0:T(8,128)} %copy.36, bf16[1,1,512,3584]{2,3,1,0:T(8,128)(2,1)S(1)} %copy-done.2), kind=kLoop, calls=%fused_computation.35 | loop fusion | flops 7340032 | bytes 22020096 | tf_op jit(solution)/shard_map/convert_element_type | solution.py:84
  271.2 76.9 %collective-permute-done = bf16[1,1,512,3584]{2,3,1,0:T(8,128)(2,1)} collective-permute-done((bf16[1,1,512,3584]{2,3,1,0:T(8,128)(2,1)}, bf16[1,1,512,3584]{2,3,1,0:T(8,128)(2,1)}, u32[]{:S(2)}, u32[]{:S(2)}) %collective-permute-start) | collective-permute-done | bytes 3670048 | tf_op jit(solution)/shard_map/ppermute | solution.py:18
  348.2 5.9 %copy.37 = bf16[1,1,512,3584]{3,2,1,0:T(8,128)(2,1)} copy(bf16[1,1,512,3584]{2,3,1,0:T(8,128)(2,1)} %collective-permute-done) | data formatting | bytes 7340032
  (195 shorter events, 107.3 us)
Async XLA Ops:
  7.2 64.8 %copy-start = (bf16[1,1,512,512]{3,2,1,0:T(8,128)(2,1)S(1)}, bf16[1,1,512,512]{3,2,1,0:T(8,128)(2,1)}, u32[]{:S(2)}) copy-start(bf16[1,1,512,512]{3,2,1,0:T(8,128)(2,1)} %param.18) | copy-start | bytes 1572868
  7.2 6.7 %copy-start.5 = (f32[1,3584]{1,0:T(1,128)S(1)}, f32[1,3584]{1,0:T(1,128)}, u32[]{:S(2)}) copy-start(f32[1,3584]{1,0:T(1,128)} %param.14) | copy-start | bytes 43012
  7.2 53.5 %all-gather.6.cloned.1.call-start = ((), (), s32[]{:S(2)}) async-start(), calls=%async_computation.4 | async-start | bytes 3899392 | tf_op jit(solution)/shard_map/all_gather | solution.py:63
  7.9 87.9 %all-gather.4.cloned.1.call-start = ((), (), s32[]{:S(2)}) async-start(), calls=%async_computation.2 | async-start | bytes 2621440 | tf_op jit(solution)/shard_map/all_gather | solution.py:66
  16.8 50.2 %copy-start.4 = (bf16[1,1,512,28]{2,3,1,0:T(8,128)(2,1)S(1)}, bf16[1,1,512,28]{2,3,1,0:T(8,128)(2,1)}, u32[]{:S(2)}) copy-start(bf16[1,1,512,28]{2,3,1,0:T(8,128)(2,1)} %param.19) | copy-start | bytes 86020
  67.0 200.9 %reduce-scatter.7.cloned.1.call-start = ((), (), s32[]{:S(2)}) async-start(), calls=%async_computation.5 | async-start | bytes 1949696
  71.9 197.6 %reduce-scatter.5.cloned.1.call-start = ((), (), s32[]{:S(2)}) async-start(), calls=%async_computation.3 | async-start | bytes 7798784 | tf_op jit(solution)/shard_map/reduce_scatter | solution.py:93
  79.4 6.4 %copy-start.6 = (bf16[1,28,3584]{2,1,0:T(8,128)(2,1)S(1)}, bf16[1,28,3584]{2,1,0:T(8,128)(2,1)}, u32[]{:S(2)}) copy-start(bf16[1,28,3584]{2,1,0:T(8,128)(2,1)} %param.16) | copy-start | bytes 602116
  244.5 8.4 %copy-start.3 = (f32[512,28]{0,1:T(8,128)S(1)}, f32[512,28]{0,1:T(8,128)}, u32[]{:S(2)}) copy-start(f32[512,28]{0,1:T(8,128)} %fusion.48) | copy-start | bytes 172036
  252.9 3.9 %copy-start.2 = (bf16[1,1,512,3584]{2,3,1,0:T(8,128)(2,1)S(1)}, bf16[1,1,512,3584]{2,3,1,0:T(8,128)(2,1)}, u32[]{:S(2)}) copy-start(bf16[1,1,512,3584]{2,3,1,0:T(8,128)(2,1)} %copy.34) | copy-start | bytes 11010052
  256.8 97.3 %copy-start.1 = (bf16[1,1,512,512]{3,2,1,0:T(8,128)(2,1)S(1)}, bf16[1,1,512,512]{3,2,1,0:T(8,128)(2,1)}, u32[]{:S(2)}) copy-start(bf16[1,1,512,512]{3,2,1,0:T(8,128)(2,1)} %param.18) | copy-start | bytes 1572868
  266.4 81.8 %collective-permute-start = (bf16[1,1,512,3584]{2,3,1,0:T(8,128)(2,1)}, bf16[1,1,512,3584]{2,3,1,0:T(8,128)(2,1)}, u32[]{:S(2)}, u32[]{:S(2)}) collective-permute-start(bf16[1,1,512,3584]{2,3,1,0:T(8,128)(2,1)} %add_convert_fusion), channel_id=1, source_target_pairs={{16,0},{0,16},{17,1},{1,17},{18,2},{2,18},{19,3},{3,19},{20,4},{4,... | collective-permute-start | bytes 11010056 | tf_op jit(solution)/shard_map/ppermute | solution.py:18
Sparse Core Ops, SparseCore 0:
  10.3 50.3 all-gather.5
  67.1 21.2 all-gather.3
  92.1 60.6 reduce-scatter.6
  156.7 90.6 reduce-scatter.4
where the time goes:
time: 363 us; the launch traced here: 361 us
  waiting for transfers between devices  122 us (34%)
  local copies, waits for them, and re-layouts  105 us (29%)
  other arithmetic  62.2 us (17%)
  matrix products  50.9 us (14%)
  between operations  13.8 us (4%)
  loops' own time  5.53 us (2%)
    ppermute x1, waiting for transfers between devices, passed_along(): return lax.ppermute(block, axis, route)  76.9 us
    all_gather x1, waiting for transfers between devices, per_device(): lax.all_gather(kv_weight[0], ('ctx', 'dp'), axis=0, tiled=True)  43.9 us
    gather x8, local copies, waits for them, and re-layouts, attend_block(): key_tiles = jnp.take(key_rows, chosen, axis=0).reshape(SEL * BLOCK, KVH, HD)  22.8 us
    dot_general x8, matrix products, attend_block(): jnp.einsum('gjqk,kgd->qgjd', weights_low, value_tiles, preferred_element_...  16.2 us
    reduce_sum x8, other arithmetic, attend_block(): denominator = jnp.sum(weights, axis=-1)  15.4 us
    unnamed x17, local copies, waits for them, and re-layouts  13.5 us
    dynamic_slice x16, local copies, waits for them, and re-layouts, per_device(): lax.map(lambda packed: attend_block(packed, key_rows, value_rows), (norme...  13.4 us
    gather x8, local copies, waits for them, and re-layouts, attend_block(): jnp.take(value_rows, chosen, axis=0).reshape(SEL * BLOCK, KVH, HD)  12.8 us
  transfers between devices with their start and end apart: 5, of which 2 were waited for; matrix products, arithmetic and copies ran while one was open for 57% of the time, Pallas kernels for 0%

commit v1 on v0

--- a/solution.py
+++ b/solution.py
@@ -10,6 +10,28 @@
 BLOCK = 64
 SEL = 16
 epsilon = 1e-06
+
+
+def in_order(pieces, dim):
+    pieces = jnp.moveaxis(pieces, 0, dim)
+    shape = pieces.shape
+    return pieces.reshape(*shape[:dim], shape[dim] * shape[dim + 1], *shape[dim + 2 :])
+
+
+def collect(array, axis, dim):
+    count = lax.axis_size(axis)
+    pairs = [(i, (i + 1) % count) for i in range(count)]
+    back = [(b, a) for a, b in pairs]
+    lower, upper = ([], [])
+    for step in range(count - 1):
+        if step % 2 == 0:
+            lower.append(lax.ppermute(lower[-1] if lower else array, axis, pairs))
+        else:
+            upper.append(lax.ppermute(upper[-1] if upper else array, axis, back))
+    blocks = jnp.stack([*lower[::-1], array, *upper])
+    shift = lax.axis_index(axis) - len(lower)
+    blocks = blocks[(jnp.arange(count) - shift) % count]
+    return in_order(blocks, dim)
 
 
 def passed_along(block, axis, distance):
@@ -59,9 +81,7 @@
         * norm_gain[0]
     ).astype(jnp.bfloat16)
     projected = jnp.dot(
-        normed,
-        lax.all_gather(kv_weight[0], ("ctx", "dp"), axis=0, tiled=True),
-        preferred_element_type=jnp.float32,
+        normed, collect(kv_weight[0], ("ctx", "dp"), 0), preferred_element_type=jnp.float32
     ).astype(jnp.bfloat16)
     sequence_kv = lax.all_gather(projected, "ctx", axis=0, tiled=True)
     half_width = KVH * HD

time: 363 us -> 418 us (1.15)
  starting transfers between devices: 1.66 us -> 32 us
  local copies, waits for them, and re-layouts: 105 us -> 124 us
    ppermute x0 -> x15, waiting for transfers between devices: none -> 47.5 us  [the longest x8 31.6 us: collect(): lower.append(lax.ppermute(lower[-1] if lower else array, axis, pairs))]
    all_gather x1 -> x0, waiting for transfers between devices: 43.9 us -> none  [per_device(): lax.all_gather(kv_weight[0], ('ctx', 'dp'), axis=0, tiled=True)]
    ppermute x0 -> x15, starting transfers between devices: none -> 27 us  [the longest x7 22 us: collect(): upper.append(lax.ppermute(upper[-1] if upper else array, axis, back))]
    unnamed x17 -> x34, local copies, waits for them, and re-layouts: 13.5 us -> 26 us
    gather x0 -> x1, local copies, waits for them, and re-layouts: none -> 4.66 us  [collect(): blocks = blocks[(jnp.arange(count) - shift) % count]]
  transfers between devices with their start and end apart: 5 -> 19, of which waited for: 2 -> 13; matrix products, arithmetic and copies ran while one was open for 57% -> 54% of each run, Pallas kernels for 0% -> 0%
where the time goes in v1:
time: 418 us; the launch traced here: 416 us
  waiting for transfers between devices  126 us (30%)
  local copies, waits for them, and re-layouts  124 us (30%)
  other arithmetic  62.3 us (15%)
  matrix products  50.7 us (12%)
  starting transfers between devices  32 us (8%)
  between operations  15.6 us (4%)
  loops' own time  6.2 us (1%)
    ppermute x1, waiting for transfers between devices, passed_along(): return lax.ppermute(block, axis, route)  78 us
    ppermute x8, waiting for transfers between devices, collect(): lower.append(lax.ppermute(lower[-1] if lower else array, axis, pairs))  31.6 us
    unnamed x34, local copies, waits for them, and re-layouts  26 us
    gather x8, local copies, waits for them, and re-layouts, attend_block(): key_tiles = jnp.take(key_rows, chosen, axis=0).reshape(SEL * BLOCK, KVH, HD)  23 us
    ppermute x7, starting transfers between devices, collect(): upper.append(lax.ppermute(upper[-1] if upper else array, axis, back))  22 us
    dot_general x8, matrix products, attend_block(): jnp.einsum('gjqk,kgd->qgjd', weights_low, value_tiles, preferred_element_...  16.2 us
    ppermute x7, waiting for transfers between devices, collect(): upper.append(lax.ppermute(upper[-1] if upper else array, axis, back))  15.9 us
    reduce_sum x8, other arithmetic, attend_block(): denominator = jnp.sum(weights, axis=-1)  15.4 us
  transfers between devices with their start and end apart: 19, of which 13 were waited for; matrix products, arithmetic and copies ran while one was open for 54% of the time, Pallas kernels for 0%

profile of v1, /device:TPU:0, one launch (start us, length us, event | category | flops | bytes accessed | tf_op | source)
XLA Modules:
  0.0 415.9 jit_solution(5364855936315450209)
XLA Ops:
  8.1 3.1 collective-permute-start
  11.2 7.9 %collective-permute-done = bf16[224,512]{1,0:T(8,128)(2,1)S(1)} collective-permute-done((bf16[224,512]{1,0:T(8,128)(2,1)}, bf16[224,512]{1,0:T(8,128)(2,1)S(1)}, u32[]{:S(2)}, u32[]{:S(2)}) %collective-permute-start) | collective-permute-done | bytes 229408 | tf_op jit(solution)/shard_map/ppermute | solution.py:28
  19.1 4.4 %collective-permute-start.8 = (bf16[224,512]{1,0:T(8,128)(2,1)}, bf16[224,512]{1,0:T(8,128)(2,1)S(1)}, u32[]{:S(2)}, u32[]{:S(2)}) collective-permute-start(bf16[224,512]{1,0:T(8,128)(2,1)} %bitcast.124), channel_id=1, source_target_pairs={{1,0},{2,1},{3,2},{4,3},{5,4},{6,5},{7,6},{8,7},{9,8},{10,9},{11,1... | collective-permute-start | bytes 688136 | tf_op jit(solution)/shard_map/ppermute | solution.py:30
  23.5 6.0 %collective-permute-done.1 = bf16[224,512]{1,0:T(8,128)(2,1)S(1)} collective-permute-done((bf16[224,512]{1,0:T(8,128)(2,1)S(1)}, bf16[224,512]{1,0:T(8,128)(2,1)S(1)}, u32[]{:S(2)}, u32[]{:S(2)}) %collective-permute-start.1) | collective-permute-done | bytes 229408 | tf_op jit(solution)/shard_map/ppermute | solution.py:28
  34.6 5.5 %collective-permute-done.2 = bf16[224,512]{1,0:T(8,128)(2,1)S(1)} collective-permute-done((bf16[224,512]{1,0:T(8,128)(2,1)S(1)}, bf16[224,512]{1,0:T(8,128)(2,1)S(1)}, u32[]{:S(2)}, u32[]{:S(2)}) %collective-permute-start.2) | collective-permute-done | bytes 229408 | tf_op jit(solution)/shard_map/ppermute | solution.py:28
  40.2 4.1 collective-permute-done.9
  45.2 5.5 %collective-permute-done.3 = bf16[224,512]{1,0:T(8,128)(2,1)S(1)} collective-permute-done((bf16[224,512]{1,0:T(8,128)(2,1)S(1)}, bf16[224,512]{1,0:T(8,128)(2,1)S(1)}, u32[]{:S(2)}, u32[]{:S(2)}) %collective-permute-start.3) | collective-permute-done | bytes 229408 | tf_op jit(solution)/shard_map/ppermute | solution.py:28
  50.8 5.9 %collective-permute-done.10 = bf16[224,512]{1,0:T(8,128)(2,1)S(1)} collective-permute-done((bf16[224,512]{1,0:T(8,128)(2,1)S(1)}, bf16[224,512]{1,0:T(8,128)(2,1)S(1)}, u32[]{:S(2)}, u32[]{:S(2)}) %collective-permute-start.10) | collective-permute-done | bytes 229408 | tf_op jit(solution)/shard_map/ppermute | solution.py:30
  56.7 4.7 %collective-permute-done.4 = bf16[224,512]{1,0:T(8,128)(2,1)S(1)} collective-permute-done((bf16[224,512]{1,0:T(8,128)(2,1)S(1)}, bf16[224,512]{1,0:T(8,128)(2,1)S(1)}, u32[]{:S(2)}, u32[]{:S(2)}) %collective-permute-start.4) | collective-permute-done | bytes 229408 | tf_op jit(solution)/shard_map/ppermute | solution.py:28
  61.4 5.9 %copy.34 = bf16[1,1,512,3584]{2,3,1,0:T(8,128)(2,1)} copy(bf16[1,1,512,3584]{3,2,1,0:T(8,128)(2,1)} %param.12) | data formatting | bytes 7340032 | tf_op args[0]
  67.3 4.5 %collective-permute-start.12 = (bf16[224,512]{1,0:T(8,128)(2,1)S(1)}, bf16[224,512]{1,0:T(8,128)(2,1)S(1)}, u32[]{:S(2)}, u32[]{:S(2)}) collective-permute-start(bf16[224,512]{1,0:T(8,128)(2,1)S(1)} %collective-permute-done.11), channel_id=1, source_target_pairs={{1,0},{2,1},{3,2},{4,3},{5,4},{6,5},{7,6},{8,7},{9,8},{10,9},{11,1... | collective-permute-start | bytes 688136 | tf_op jit(solution)/shard_map/ppermute | solution.py:30
  71.8 2.9 multiply_reduce_fusion
  75.5 4.6 %collective-permute-start.13 = (bf16[224,512]{1,0:T(8,128)(2,1)S(1)}, bf16[224,512]{1,0:T(8,128)(2,1)S(1)}, u32[]{:S(2)}, u32[]{:S(2)}) collective-permute-start(bf16[224,512]{1,0:T(8,128)(2,1)S(1)} %collective-permute-done.12), channel_id=1, source_target_pairs={{1,0},{2,1},{3,2},{4,3},{5,4},{6,5},{7,6},{8,7},{9,8},{10,9},{11,1... | collective-permute-start | bytes 688136 | tf_op jit(solution)/shard_map/ppermute | solution.py:30
  82.5 2.9 collective-permute-done.13
  85.4 4.7 %collective-permute-start.14 = (bf16[224,512]{1,0:T(8,128)(2,1)S(1)}, bf16[224,512]{1,0:T(8,128)(2,1)S(1)}, u32[]{:S(2)}, u32[]{:S(2)}) collective-permute-start(bf16[224,512]{1,0:T(8,128)(2,1)S(1)} %collective-permute-done.13), channel_id=1, source_target_pairs={{1,0},{2,1},{3,2},{4,3},{5,4},{6,5},{7,6},{8,7},{9,8},{10,9},{11,1... | collective-permute-start | bytes 688136 | tf_op jit(solution)/shard_map/ppermute | solution.py:30
  104.7 4.7 %gather_fusion.2 = bf16[16,224,512]{2,1,0:T(8,128)(2,1)} fusion(bf16[16,224,512]{2,1,0:T(8,128)(2,1)} %bitcast_dynamic-update-slice_fusion, s32[1024]{0:T(1024)S(1)} %pad_clamp_fusion.1), kind=kCustom, calls=%fused_computation.2 | custom fusion | bytes 7340096 | tf_op jit(solution)/shard_map/gather | solution.py:33
  109.3 6.2 %convolution_convert_fusion = bf16[512,512]{1,0:T(8,128)(2,1)} fusion(bf16[3584,512]{1,0:T(8,128)(2,1)} %bitcast.121, bf16[1,1,512,3584]{2,3,1,0:T(8,128)(2,1)} %copy.34, f32[3584]{0:T(1024)S(1)} %reduce.1, f32[512]{0:T(512)S(1)} %add_rsqrt_fusion), kind=kOutput, calls=%fused_computation.40 | convolution fusion | flops 1886650368 | bytes 7880704 | tf_op jit(solution)/shard_map/dot_general | solution.py:83
  115.6 4.9 %convolution_bitcast_fusion = f32[3584,28]{1,0:T(8,128)} fusion(bf16[1,1,512,3584]{3,2,1,0:T(8,128)(2,1)} %param.17, bf16[1,1,512,28]{2,3,1,0:T(8,128)(2,1)S(1)} %copy-done.5), kind=kOutput, calls=%fused_computation.35 | convolution fusion | flops 102760448 | bytes 4100096
  120.6 7.2 %fusion.20 = f32[3584,512]{1,0:T(8,128)} fusion(bf16[1,1,512,3584]{3,2,1,0:T(8,128)(2,1)} %param.17, bf16[1,1,512,512]{3,2,1,0:T(8,128)(2,1)S(1)} %copy-done), kind=kOutput, calls=%fused_computation.38 | convolution fusion | flops 1879048192 | bytes 11534336 | tf_op jit(solution)/shard_map/dot_general | solution.py:107
  127.9 6.4 %copy.35 = f32[1,1,512,3584]{3,2,1,0:T(8,128)} copy(bf16[1,1,512,3584]{2,3,1,0:T(8,128)(2,1)} %copy.34) | data formatting | bytes 11010048 | tf_op jit(solution)/shard_map/convert_element_type | solution.py:77
  134.3 4.0 fusion.24
  138.3 6.3 %multiply_convert_fusion = bf16[8,64,3584]{2,1,0:T(8,128)(2,1)} fusion(f32[8,64,3584]{2,1,0:T(8,128)} %bitcast.117, f32[3584]{0:T(1024)S(1)} %reduce.1, f32[8,64]{1,0:T(8,128)S(1)} %rsqrt.13), kind=kLoop, calls=%fused_computation.32 | loop fusion | flops 5505024 | bytes 11026432 | tf_op jit(solution)/shard_map/convert_element_type | solution.py:82
  149.7 144.7 %while.10 = (s32[]{:T(128)}, f32[8,64,3584]{2,1,0:T(8,128)}, s32[8,16]{1,0:T(8,128)}, bf16[32,64,2,128]{3,2,1,0:T(2,128)(2,1)S(1)}, s32[8]{0:T(128)S(1)}, /*inde...) while((s32[]{:T(128)}, f32[8,64,3584]{2,1,0:T(8,128)}, ...), condition=%wide.region_4.6_spmd, body=%wide.region_1.5_spmd.sunk | while | flops 960592640 | bytes 36303624 | solution.py:98
  206.2 2.9 gather_fusion.1
  242.3 2.9 gather_fusion.1
  260.4 3.1 gather_fusion.1
  294.4 8.4 %copy.36 = f32[1,1,512,3584]{2,3,1,0:T(8,128)} copy(f32[1,1,512,3584]{3,2,1,0:T(8,128)} %bitcast.120) | data formatting | bytes 14680064 | tf_op jit(solution)/shard_map/reshape | solution.py:102
  302.8 4.0 mul.86
  306.8 9.5 %add_convert_fusion = bf16[1,1,512,3584]{2,3,1,0:T(8,128)(2,1)} fusion(f32[1,1,512,3584]{2,3,1,0:T(8,128)} %bitcast.118, f32[1,1,512,3584]{2,3,1,0:T(8,128)} %copy.36, bf16[1,1,512,3584]{2,3,1,0:T(8,128)(2,1)S(1)} %copy-done.2), kind=kLoop, calls=%fused_computation.31 | loop fusion | flops 7340032 | bytes 22020096 | tf_op jit(solution)/shard_map/convert_element_type | solution.py:104
  316.3 4.8 %collective-permute-start.15 = (bf16[1,1,512,3584]{2,3,1,0:T(8,128)(2,1)}, bf16[1,1,512,3584]{2,3,1,0:T(8,128)(2,1)}, u32[]{:S(2)}, u32[]{:S(2)}) collective-permute-start(bf16[1,1,512,3584]{2,3,1,0:T(8,128)(2,1)} %add_convert_fusion), channel_id=1, source_target_pairs={{16,0},{0,16},{17,1},{1,17},{18,2},{2,18},{19,3},{3,19},{20,4},{4,... | collective-permute-start | bytes 11010056 | tf_op jit(solution)/shard_map/ppermute | solution.py:40
  322.8 78.0 %collective-permute-done.15 = bf16[1,1,512,3584]{2,3,1,0:T(8,128)(2,1)} collective-permute-done((bf16[1,1,512,3584]{2,3,1,0:T(8,128)(2,1)}, bf16[1,1,512,3584]{2,3,1,0:T(8,128)(2,1)}, u32[]{:S(2)}, u32[]{:S(2)}) %collective-permute-start.15) | collective-permute-done | bytes 3670048 | tf_op jit(solution)/shard_map/ppermute | solution.py:40
  400.8 5.9 %copy.37 = bf16[1,1,512,3584]{3,2,1,0:T(8,128)(2,1)} copy(bf16[1,1,512,3584]{2,3,1,0:T(8,128)(2,1)} %collective-permute-done.15) | data formatting | bytes 7340032
  (243 shorter events, 162.3 us)
Async XLA Ops:
  8.0 112.6 %copy-start = (bf16[1,1,512,512]{3,2,1,0:T(8,128)(2,1)S(1)}, bf16[1,1,512,512]{3,2,1,0:T(8,128)(2,1)}, u32[]{:S(2)}) copy-start(bf16[1,1,512,512]{3,2,1,0:T(8,128)(2,1)} %param.18) | copy-start | bytes 1572868
  8.0 136.6 %all-gather.2.cloned.1.call-start = ((), (), s32[]{:S(2)}) async-start(), calls=%async_computation.2 | async-start | bytes 2621440 | tf_op jit(solution)/shard_map/all_gather | solution.py:86
  8.1 11.0 %collective-permute-start = (bf16[224,512]{1,0:T(8,128)(2,1)}, bf16[224,512]{1,0:T(8,128)(2,1)S(1)}, u32[]{:S(2)}, u32[]{:S(2)}) collective-permute-start(bf16[224,512]{1,0:T(8,128)(2,1)} %bitcast.123), channel_id=1, source_target_pairs={{0,1},{1,2},{2,3},{3,4},{4,5},{5,6},{6,7},{7,8},{8,9},{9,10},{10,1... | collective-permute-start | bytes 688136 | tf_op jit(solution)/shard_map/ppermute | solution.py:28
  19.1 10.5 %collective-permute-start.1 = (bf16[224,512]{1,0:T(8,128)(2,1)S(1)}, bf16[224,512]{1,0:T(8,128)(2,1)S(1)}, u32[]{:S(2)}, u32[]{:S(2)}) collective-permute-start(bf16[224,512]{1,0:T(8,128)(2,1)S(1)} %collective-permute-done), channel_id=1, source_target_pairs={{0,1},{1,2},{2,3},{3,4},{4,5},{5,6},{6,7},{7,8},{8,9},{9,10},{10,1... | collective-permute-start | bytes 688136 | tf_op jit(solution)/shard_map/ppermute | solution.py:28
  19.1 12.8 %collective-permute-start.8 = (bf16[224,512]{1,0:T(8,128)(2,1)}, bf16[224,512]{1,0:T(8,128)(2,1)S(1)}, u32[]{:S(2)}, u32[]{:S(2)}) collective-permute-start(bf16[224,512]{1,0:T(8,128)(2,1)} %bitcast.124), channel_id=1, source_target_pairs={{1,0},{2,1},{3,2},{4,3},{5,4},{6,5},{7,6},{8,7},{9,8},{10,9},{11,1... | collective-permute-start | bytes 688136 | tf_op jit(solution)/shard_map/ppermute | solution.py:30
  29.5 10.6 %collective-permute-start.2 = (bf16[224,512]{1,0:T(8,128)(2,1)S(1)}, bf16[224,512]{1,0:T(8,128)(2,1)S(1)}, u32[]{:S(2)}, u32[]{:S(2)}) collective-permute-start(bf16[224,512]{1,0:T(8,128)(2,1)S(1)} %collective-permute-done.1), channel_id=1, source_target_pairs={{0,1},{1,2},{2,3},{3,4},{4,5},{5,6},{6,7},{7,8},{8,9},{9,10},{10,1... | collective-permute-start | bytes 688136 | tf_op jit(solution)/shard_map/ppermute | solution.py:28
  31.8 12.4 %collective-permute-start.9 = (bf16[224,512]{1,0:T(8,128)(2,1)S(1)}, bf16[224,512]{1,0:T(8,128)(2,1)S(1)}, u32[]{:S(2)}, u32[]{:S(2)}) collective-permute-start(bf16[224,512]{1,0:T(8,128)(2,1)S(1)} %collective-permute-done.8), channel_id=1, source_target_pairs={{1,0},{2,1},{3,2},{4,3},{5,4},{6,5},{7,6},{8,7},{9,8},{10,9},{11,1... | collective-permute-start | bytes 688136 | tf_op jit(solution)/shard_map/ppermute | solution.py:30
  40.2 10.6 %collective-permute-start.3 = (bf16[224,512]{1,0:T(8,128)(2,1)S(1)}, bf16[224,512]{1,0:T(8,128)(2,1)S(1)}, u32[]{:S(2)}, u32[]{:S(2)}) collective-permute-start(bf16[224,512]{1,0:T(8,128)(2,1)S(1)} %collective-permute-done.2), channel_id=1, source_target_pairs={{0,1},{1,2},{2,3},{3,4},{4,5},{5,6},{6,7},{7,8},{8,9},{9,10},{10,1... | collective-permute-start | bytes 688136 | tf_op jit(solution)/shard_map/ppermute | solution.py:28
  44.2 12.4 %collective-permute-start.10 = (bf16[224,512]{1,0:T(8,128)(2,1)S(1)}, bf16[224,512]{1,0:T(8,128)(2,1)S(1)}, u32[]{:S(2)}, u32[]{:S(2)}) collective-permute-start(bf16[224,512]{1,0:T(8,128)(2,1)S(1)} %collective-permute-done.9), channel_id=1, source_target_pairs={{1,0},{2,1},{3,2},{4,3},{5,4},{6,5},{7,6},{8,7},{9,8},{10,9},{11,1... | collective-permute-start | bytes 688136 | tf_op jit(solution)/shard_map/ppermute | solution.py:30
  50.8 10.6 %collective-permute-start.4 = (bf16[224,512]{1,0:T(8,128)(2,1)S(1)}, bf16[224,512]{1,0:T(8,128)(2,1)S(1)}, u32[]{:S(2)}, u32[]{:S(2)}) collective-permute-start(bf16[224,512]{1,0:T(8,128)(2,1)S(1)} %collective-permute-done.3), channel_id=1, source_target_pairs={{0,1},{1,2},{2,3},{3,4},{4,5},{5,6},{6,7},{7,8},{8,9},{9,10},{10,1... | collective-permute-start | bytes 688136 | tf_op jit(solution)/shard_map/ppermute | solution.py:28
  56.7 10.7 %collective-permute-start.11 = (bf16[224,512]{1,0:T(8,128)(2,1)S(1)}, bf16[224,512]{1,0:T(8,128)(2,1)S(1)}, u32[]{:S(2)}, u32[]{:S(2)}) collective-permute-start(bf16[224,512]{1,0:T(8,128)(2,1)S(1)} %collective-permute-done.10), channel_id=1, source_target_pairs={{1,0},{2,1},{3,2},{4,3},{5,4},{6,5},{7,6},{8,7},{9,8},{10,9},{11,1... | collective-permute-start | bytes 688136 | tf_op jit(solution)/shard_map/ppermute | solution.py:30
  61.4 10.5 %collective-permute-start.5 = (bf16[224,512]{1,0:T(8,128)(2,1)S(1)}, bf16[224,512]{1,0:T(8,128)(2,1)S(1)}, u32[]{:S(2)}, u32[]{:S(2)}) collective-permute-start(bf16[224,512]{1,0:T(8,128)(2,1)S(1)} %collective-permute-done.4), channel_id=1, source_target_pairs={{0,1},{1,2},{2,3},{3,4},{4,5},{5,6},{6,7},{7,8},{8,9},{9,10},{10,1... | collective-permute-start | bytes 688136 | tf_op jit(solution)/shard_map/ppermute | solution.py:28
  67.3 15.2 %copy-start.6 = (f32[1,3584]{1,0:T(1,128)S(1)}, f32[1,3584]{1,0:T(1,128)}, u32[]{:S(2)}) copy-start(f32[1,3584]{1,0:T(1,128)} %param.14) | copy-start | bytes 43012
  67.3 31.7 %copy-start.3 = (bf16[1,224,512]{2,1,0:T(8,128)(2,1)S(1)}, bf16[1,224,512]{2,1,0:T(8,128)(2,1)}, u32[]{:S(2)}) copy-start(bf16[1,224,512]{2,1,0:T(8,128)(2,1)} %param.15) | copy-start | bytes 688132
  67.3 8.1 %collective-permute-start.12 = (bf16[224,512]{1,0:T(8,128)(2,1)S(1)}, bf16[224,512]{1,0:T(8,128)(2,1)S(1)}, u32[]{:S(2)}, u32[]{:S(2)}) collective-permute-start(bf16[224,512]{1,0:T(8,128)(2,1)S(1)} %collective-permute-done.11), channel_id=1, source_target_pairs={{1,0},{2,1},{3,2},{4,3},{5,4},{6,5},{7,6},{8,7},{9,8},{10,9},{11,1... | collective-permute-start | bytes 688136 | tf_op jit(solution)/shard_map/ppermute | solution.py:30
  71.8 8.7 %collective-permute-start.6 = (bf16[224,512]{1,0:T(8,128)(2,1)S(1)}, bf16[224,512]{1,0:T(8,128)(2,1)}, u32[]{:S(2)}, u32[]{:S(2)}) collective-permute-start(bf16[224,512]{1,0:T(8,128)(2,1)S(1)} %collective-permute-done.5), channel_id=1, source_target_pairs={{0,1},{1,2},{2,3},{3,4},{4,5},{5,6},{6,7},{7,8},{8,9},{9,10},{10,1... | collective-permute-start | bytes 688136 | tf_op jit(solution)/shard_map/ppermute | solution.py:28
  75.5 9.9 %collective-permute-start.13 = (bf16[224,512]{1,0:T(8,128)(2,1)S(1)}, bf16[224,512]{1,0:T(8,128)(2,1)S(1)}, u32[]{:S(2)}, u32[]{:S(2)}) collective-permute-start(bf16[224,512]{1,0:T(8,128)(2,1)S(1)} %collective-permute-done.12), channel_id=1, source_target_pairs={{1,0},{2,1},{3,2},{4,3},{5,4},{6,5},{7,6},{8,7},{9,8},{10,9},{11,1... | collective-permute-start | bytes 688136 | tf_op jit(solution)/shard_map/ppermute | solution.py:30
  80.6 10.9 %collective-permute-start.7 = (bf16[224,512]{1,0:T(8,128)(2,1)}, bf16[224,512]{1,0:T(8,128)(2,1)}, u32[]{:S(2)}, u32[]{:S(2)}) collective-permute-start(bf16[224,512]{1,0:T(8,128)(2,1)} %collective-permute-done.6), channel_id=1, source_target_pairs={{0,1},{1,2},{2,3},{3,4},{4,5},{5,6},{6,7},{7,8},{8,9},{9,10},{10,1... | collective-permute-start | bytes 688136 | tf_op jit(solution)/shard_map/ppermute | solution.py:28
  85.4 18.6 %collective-permute-start.14 = (bf16[224,512]{1,0:T(8,128)(2,1)S(1)}, bf16[224,512]{1,0:T(8,128)(2,1)S(1)}, u32[]{:S(2)}, u32[]{:S(2)}) collective-permute-start(bf16[224,512]{1,0:T(8,128)(2,1)S(1)} %collective-permute-done.13), channel_id=1, source_target_pairs={{1,0},{2,1},{3,2},{4,3},{5,4},{6,5},{7,6},{8,7},{9,8},{10,9},{11,1... | collective-permute-start | bytes 688136 | tf_op jit(solution)/shard_map/ppermute | solution.py:30
  109.3 6.3 %copy-start.5 = (bf16[1,1,512,28]{2,3,1,0:T(8,128)(2,1)S(1)}, bf16[1,1,512,28]{2,3,1,0:T(8,128)(2,1)}, u32[]{:S(2)}) copy-start(bf16[1,1,512,28]{2,3,1,0:T(8,128)(2,1)} %param.19) | copy-start | bytes 86020
  115.6 205.5 %reduce-scatter.7.cloned.1.call-start = ((), (), s32[]{:S(2)}) async-start(), calls=%async_computation.4 | async-start | bytes 1949696
  120.5 286.2 %reduce-scatter.5.cloned.1.call-start = ((), (), s32[]{:S(2)}) async-start(), calls=%async_computation.3 | async-start | bytes 7798784 | tf_op jit(solution)/shard_map/reduce_scatter | solution.py:113
  127.9 6.4 %copy-start.7 = (bf16[1,28,3584]{2,1,0:T(8,128)(2,1)S(1)}, bf16[1,28,3584]{2,1,0:T(8,128)(2,1)}, u32[]{:S(2)}) copy-start(bf16[1,28,3584]{2,1,0:T(8,128)(2,1)} %param.16) | copy-start | bytes 602116
  294.4 8.4 %copy-start.4 = (f32[512,28]{0,1:T(8,128)S(1)}, f32[512,28]{0,1:T(8,128)}, u32[]{:S(2)}) copy-start(f32[512,28]{0,1:T(8,128)} %fusion.24) | copy-start | bytes 172036
  302.8 4.0 copy-start.2
  316.3 84.5 %collective-permute-start.15 = (bf16[1,1,512,3584]{2,3,1,0:T(8,128)(2,1)}, bf16[1,1,512,3584]{2,3,1,0:T(8,128)(2,1)}, u32[]{:S(2)}, u32[]{:S(2)}) collective-permute-start(bf16[1,1,512,3584]{2,3,1,0:T(8,128)(2,1)} %add_convert_fusion), channel_id=1, source_target_pairs={{16,0},{0,16},{17,1},{1,17},{18,2},{2,18},{19,3},{3,19},{20,4},{4,... | collective-permute-start | bytes 11010056 | tf_op jit(solution)/shard_map/ppermute | solution.py:40
  321.1 87.3 %copy-start.1 = (bf16[1,1,512,512]{3,2,1,0:T(8,128)(2,1)S(1)}, bf16[1,1,512,512]{3,2,1,0:T(8,128)(2,1)}, u32[]{:S(2)}) copy-start(bf16[1,1,512,512]{3,2,1,0:T(8,128)(2,1)} %param.18) | copy-start | bytes 1572868
Sparse Core Ops, SparseCore 0:
  115.7 26.2 all-gather.1
Sparse Core Ops, SparseCore 1:
  120.6 64.5 reduce-scatter.6
  189.0 90.3 reduce-scatter.4
